TPU v7x, 32 devices: a whole 2x2x4 slice. The times are simulated.
32 devices in a mesh: groups: 1, fsdp: 8 (over z, y), seq: 4 (over x, core), sub: 1.
Axes of the slice: x: 2, y: 2, z: 4, core: 2. Of those that a mesh axis runs over, the one named last changes fastest.
Arguments:
- tokens: bfloat16 [8, 1, 4, 128, 2048], P(('groups', 'fsdp'), 'sub', 'seq'), may hold values from -6 to 6
- frame_valid: int32 [8, 1, 4], P(('groups', 'fsdp'), 'sub'), may hold values from 0 to 1, as said below
- w_qkv: bfloat16 [2048, 3, 2048], P('fsdp', None, 'seq'), may hold values from -0.1875 to 0.1875
- w_out: bfloat16 [2048, 2048], P('seq', 'fsdp'), may hold values from -0.125 to 0.125
- w_act: bfloat16 [2048, 8192], P(None, 'fsdp'), may hold values from -0.125 to 0.125
- class_table: int32 [8192], P('fsdp'), may hold values from 0 to 120
- cam_bias: float32 [121], replicated, may hold values from -4 to 4
Outputs:
- hidden: bfloat16 [8, 1, 4, 128, 2048], P(('groups', 'fsdp'), 'sub', 'seq')
- logits: float32 [8, 1, 4, 8192], P('groups', 'sub', 'seq', 'fsdp')
Inputs may be any that keep to these rules, and one draw needn't show every extreme that they name: `frame_valid`: each window has at least one frame with value 1.
All inputs are finite; a program needn't handle non-finite values.
Results may differ from a plain program's by a relative error of at most 0.0058.
Values may be sent and summed in bfloat16 or wider, within the bound.
A program may use at most 128 MiB of HBM per device.

v0:
```python
import math

import jax
import jax.numpy as jnp
from jax import lax
from jax.sharding import PartitionSpec as P

DH = 128


def normalize(values):
    centre = jnp.mean(values, axis=-1, keepdims=True)
    spread = jnp.mean(jnp.square(values - centre), axis=-1, keepdims=True)
    return (values - centre) * lax.rsqrt(spread + 1e-05)


def per_device(tokens, frame_valid, w_qkv, w_out, w_act, class_table, cam_bias):
    windows_here = tokens.shape[0]
    frame_rows = tokens.shape[3]
    model_width = tokens.shape[4]
    own_rows = tokens[:, 0, 0].astype(jnp.float32)
    normed = normalize(own_rows).astype(jnp.bfloat16)
    gathered = lax.all_gather(normed[:, None], "seq", axis=1, tiled=True)
    frame_count = gathered.shape[1]
    span_rows = frame_count * frame_rows
    window_rows = gathered.reshape(windows_here, span_rows, model_width)
    full_qkv = lax.all_gather(w_qkv, "fsdp", axis=0, tiled=True)
    projected = jnp.einsum(
        "wsd,dcn->wscn", window_rows, full_qkv, preferred_element_type=jnp.float32
    ).astype(jnp.bfloat16)
    local_heads = full_qkv.shape[2] // DH
    projected = projected.reshape(windows_here, span_rows, 3, local_heads, DH)
    queries = projected[:, :, 0]
    keys_all = projected[:, :, 1]
    values_all = projected[:, :, 2]
    key_mask = jnp.repeat(frame_valid[:, 0].astype(jnp.float32), frame_rows, axis=1)
    score_scale = 1.0 / math.sqrt(DH)
    scores = (
        jnp.einsum("wqhe,wkhe->whqk", queries, keys_all, preferred_element_type=jnp.float32)
        * score_scale
    )
    weights = jnp.exp(scores) * key_mask[:, None, None, :]
    totals = jnp.sum(weights, axis=-1)
    mixed_heads = jnp.einsum(
        "whqk,wkhe->wqhe",
        weights.astype(jnp.bfloat16),
        values_all,
        preferred_element_type=jnp.float32,
    )
    mixed_heads = mixed_heads / jnp.transpose(totals, (0, 2, 1))[:, :, :, None]
    mixed_heads = mixed_heads.astype(jnp.bfloat16).reshape(
        windows_here, frame_count, frame_rows, local_heads * DH
    )
    frame_major = jnp.transpose(mixed_heads, (1, 0, 2, 3)).reshape(
        frame_count * windows_here * frame_rows, local_heads * DH
    )
    full_out = lax.all_gather(w_out, "fsdp", axis=1, tiled=True)
    branch = lax.psum_scatter(
        jnp.dot(frame_major, full_out, preferred_element_type=jnp.float32),
        "seq",
        scatter_dimension=0,
        tiled=True,
    )
    hidden = own_rows + branch.reshape(windows_here, frame_rows, model_width)
    hidden_out = hidden.astype(jnp.bfloat16)
    hidden_wide = lax.optimization_barrier(hidden_out).astype(jnp.float32)
    pooled = normalize(jnp.mean(hidden_wide, axis=1)).astype(jnp.bfloat16)
    camera_ids = jnp.arange(cam_bias.shape[0], dtype=jnp.int32)
    onehot = (class_table[:, None] == camera_ids[None, :]).astype(jnp.float32)
    bias_cols = jnp.dot(onehot, cam_bias, precision=lax.Precision.HIGHEST)
    logits = (
        jnp.dot(
            lax.all_gather(pooled, "fsdp", axis=0, tiled=True),
            w_act,
            preferred_element_type=jnp.float32,
        )
        + bias_cols[None, :]
    )
    hidden_shard = hidden_out.reshape(windows_here, 1, 1, frame_rows, model_width)
    logit_shard = logits.reshape(logits.shape[0], 1, 1, logits.shape[1])
    return (hidden_shard, logit_shard)


def solution(mesh):
    in_specs = (
        P(("groups", "fsdp"), "sub", "seq", None, None),
        P(("groups", "fsdp"), "sub", None),
        P("fsdp", None, "seq"),
        P("seq", "fsdp"),
        P(None, "fsdp"),
        P("fsdp"),
        P(),
    )
    out_specs = (P(("groups", "fsdp"), "sub", "seq", None, None), P("groups", "sub", "seq", "fsdp"))
    return jax.shard_map(
        per_device, mesh=mesh, in_specs=in_specs, out_specs=out_specs, check_vma=False
    )
```

profile of v0, /device:TPU:0, one launch (start us, length us, event | category | flops | bytes accessed | tf_op | source)
XLA Modules:
  0.0 282.9 jit_solution(5235049157297667890)
XLA Ops:
  7.2 1.2 convert_reduce_fusion
  8.4 1.3 fusion.17
  9.8 2.2 fusion.20
  12.0 0.0 all-gather.7.cloned.1.call-start
  12.0 2.3 copy.15
  14.3 0.0 all-gather.9.cloned.1.call-start
  14.4 0.7 all-gather.9.cloned.1.call-update
  15.1 0.1 broadcast_bitcast_fusion
  15.2 22.2 %all-gather.5.cloned.1.call-done = bf16[1,4,128,2048]{3,2,0,1:T(8,128)(2,1)} async-done(((bf16[1,1,128,2048]{3,2,0,1:T(8,128)(2,1)}), bf16[1,4,128,2048]{3,2,0,1:T(8,128)(2,1)}) %all-gather.5.cloned.1.call-update) | async-done | bytes 2097168 | tf_op jit(solution)/shard_map/all_gather | solution.py:23
  37.4 101.6 %all-gather.7.cloned.1.call-done = bf16[2048,3,512]{0,2,1:T(8,128)(2,1)} async-done(((bf16[256,3,512]{0,2,1:T(8,128)(2,1)}), bf16[2048,3,512]{0,2,1:T(8,128)(2,1)}) %all-gather.7.cloned.1.call-update) | async-done | bytes 6291472 | tf_op jit(solution)/shard_map/all_gather | solution.py:27
  139.0 6.9 %convolution_convert_fusion = bf16[512,3,512]{0,2,1:T(8,128)(2,1)S(1)} fusion(bf16[512,2048,1]{1,0,2:T(8,128)(2,1)} %bitcast.86, bf16[2048,3,512]{0,2,1:T(8,128)(2,1)} %all-gather.7.cloned.1.call-done), kind=kOutput, calls=%fused_computation.10 | convolution fusion | flops 3222011904 | bytes 9961472 | tf_op jit(solution)/shard_map/wsd,dcn->wscn/dot_general | solution.py:28
  145.8 1.1 fusion
  147.0 1.0 divide_convert_fusion
  147.9 41.6 %all-gather.9.cloned.1.call-done = bf16[512,2048]{1,0:T(8,128)(2,1)} async-done(((bf16[512,256]{1,0:T(8,128)(2,1)}), bf16[512,2048]{1,0:T(8,128)(2,1)}) %all-gather.9.cloned.1.call-update) | async-done | bytes 2097168 | tf_op jit(solution)/shard_map/all_gather | solution.py:57
  189.6 4.9 %fusion.28 = f32[512,2048]{1,0:T(8,128)} fusion(bf16[512,512]{0,1:T(8,128)(2,1)S(1)} %bitcast.83, bf16[512,2048]{1,0:T(8,128)(2,1)} %all-gather.9.cloned.1.call-done), kind=kOutput, calls=%fused_computation.43 | convolution fusion | flops 1073741824 | bytes 6815744 | tf_op jit(solution)/shard_map/dot_general | solution.py:59
  194.5 0.4 fusion.22
  194.9 42.4 %reduce-scatter.2.cloned.1.call-done = f32[128,2048]{1,0:T(8,128)} async-done(((f32[512,2048]{1,0:T(8,128)}), f32[128,2048]{1,0:T(8,128)}) %reduce-scatter.2.cloned.1.call-update) | async-done | bytes 1048592 | tf_op jit(solution)/shard_map/reduce_scatter | solution.py:58
  237.3 2.2 fusion.26
  239.5 0.1 convert_reduce_fusion.1
  239.6 0.6 multiply_reduce_fusion.1
  240.9 0.6 multiply_reduce_fusion
  242.2 30.7 %all-gather = bf16[16384]{0:T(1024)(128)(2,1)S(1)} all-gather(bf16[2048]{0:T(1024)(128)(2,1)S(1)} %multiply_convert_fusion), channel_id=2, replica_groups=mesh['groups'=1,'fsdp'=8,'seq'=4,'sub'=1] {'fsdp'}, dimensions={0}, use_global_device_ids=true | all-gather | bytes 36864 | tf_op jit(solution)/shard_map/all_gather | solution.py:73
  272.9 2.8 %fusion.9 = f32[8,1,1,1024]{3,0,2,1:T(8,128)S(1)} fusion(bf16[8,2048]{1,0:T(8,128)(2,1)S(1)} %reshape.252, bf16[2048,1024]{1,0:T(8,128)(2,1)} %param.11, f32[1024]{0:T(1024)S(1)} %bitcast.85), kind=kOutput, calls=%fused_computation.13 | convolution fusion | flops 33562624 | bytes 4263936 | tf_op jit(solution)/shard_map/dot_general | solution.py:72
  275.7 0.7 copy.19
  (18 shorter events, 0.2 us)
Async XLA Ops:
  7.2 187.3 %copy-start = (f32[121]{0:T(128)S(1)}, f32[121]{0:T(128)}, u32[]{:S(2)}) copy-start(f32[121]{0:T(128)} %param.13) | copy-start | bytes 1456
  7.2 7.9 %copy-start.3 = (s32[1,1,4]{2,1,0:T(1,128)S(1)}, s32[1,1,4]{2,1,0:T(1,128)}, u32[]{:S(2)}) copy-start(s32[1,1,4]{2,1,0:T(1,128)} %param.8) | copy-start | bytes 52
  7.2 30.2 %all-gather.5.cloned.1.call-start = ((), (), s32[]{:S(2)}) async-start(), calls=%async_computation.1 | async-start | bytes 2621440 | tf_op jit(solution)/shard_map/all_gather | solution.py:23
  12.0 127.0 %all-gather.7.cloned.1.call-start = ((), (), s32[]{:S(2)}) async-start(), calls=%async_computation.2 | async-start | bytes 7077888 | tf_op jit(solution)/shard_map/all_gather | solution.py:27
  14.3 175.2 %all-gather.9.cloned.1.call-start = ((), (), s32[]{:S(2)}) async-start(), calls=%async_computation.3 | async-start | bytes 2359296 | tf_op jit(solution)/shard_map/all_gather | solution.py:57
  15.1 222.3 %reduce-scatter.2.cloned.1.call-start = ((), (), s32[]{:S(2)}) async-start(), calls=%async_computation.4 | async-start | bytes 5242880 | tf_op jit(solution)/shard_map/reduce_scatter | solution.py:58
  189.6 4.9 %copy-start.2 = (s32[1024]{0:T(1024)S(1)}, s32[1024]{0:T(1024)}, u32[]{:S(2)}) copy-start(s32[1024]{0:T(1024)} %param.12) | copy-start | bytes 12292
  189.6 47.8 %copy-start.1 = (bf16[1,1,1,128,2048]{4,3,2,1,0:T(8,128)(2,1)S(1)}, bf16[1,1,1,128,2048]{4,3,2,1,0:T(8,128)(2,1)}, u32[]{:S(2)}) copy-start(bf16[1,1,1,128,2048]{4,3,2,1,0:T(8,128)(2,1)} %param.7) | copy-start | bytes 1572868
Sparse Core Ops, SparseCore 0:
  12.1 25.2 all-gather.4
  39.4 99.4 all-gather.6
  141.0 48.5 all-gather.8
  194.6 42.7 reduce-scatter.1
where the time goes:
time: 283 us
  waiting for transfers between devices  209 us (74%)
  blocking collectives  30.7 us (11%)
  matrix products  17.1 us (6%)
  between operations  15.2 us (5%)
  other arithmetic  8.18 us (3%)
  local copies, waits for them, and re-layouts  3.06 us (1%)
    all_gather x1, waiting for transfers between devices, per_device(): full_qkv = lax.all_gather(w_qkv, 'fsdp', axis=0, tiled=True)  102 us
    reduce_scatter x1, waiting for transfers between devices, per_device(): lax.psum_scatter(jnp.dot(frame_major, full_out, preferred_element_type=jn...  42.4 us
    all_gather x1, waiting for transfers between devices, per_device(): full_out = lax.all_gather(w_out, 'fsdp', axis=1, tiled=True)  41.6 us
    all_gather x1, blocking collectives, per_device(): lax.all_gather(pooled, 'fsdp', axis=0, tiled=True)  30.7 us
    all_gather x1, waiting for transfers between devices, per_device(): gathered = lax.all_gather(normed[:, None], 'seq', axis=1, tiled=True)  22.2 us
    dot_general x1, matrix products, per_device(): jnp.einsum('wsd,dcn->wscn', window_rows, full_qkv, preferred_element_type...  6.89 us
  transfers between devices with their start and end apart: 4, of which 4 were waited for; matrix products, arithmetic and copies ran while one was open for 4% of the time, Pallas kernels for 0%

commit v1 on v0

v1 whole, which is shorter than its diff:
```python
import functools
import math

import jax
import jax.numpy as jnp
from jax import lax
from jax.experimental import pallas as pl
from jax.experimental.pallas import tpu as pltpu
from jax.sharding import PartitionSpec as P

DH = 128
PAIR = 2
UP, DOWN, ACROSS = 0, 1, 2
LINE_QKV, PAIR_QKV, LINE_OUT = 0, 1, 2
F32 = jnp.float32
BF16 = jnp.bfloat16


def normalize(values):
    centre = jnp.mean(values, axis=-1, keepdims=True)
    shifted = values - centre
    spread = jnp.mean(jnp.square(shifted), axis=-1, keepdims=True)
    return shifted * lax.rsqrt(spread + 1e-05)


def layer_kernel(
    shards, seqs,
    tok_in, valid_ref, qkv_in, out_in, act_in, table_ref, bias_ref,
    hidden_ref, logits_ref,
    tok, nrm, own_tok, wz, wy, wo, act, acc_z, acc_y, proj, att, own_part,
    part_out, part_in, hid, col_sum, row_tile, pool_tile, pool_wide, pool_rows, bias_row,
    local_sem, send_sem, recv_sem, tok_send, tok_recv, part_send, part_recv, pool_send, pool_recv,
):
    f = lax.axis_index("fsdp")
    s = lax.axis_index("seq")
    length = shards // PAIR
    a = f // PAIR
    b = f % PAIR
    rows = tok.shape[1]
    depth = nrm.shape[2]
    cols = wo.shape[2]
    z_cols = wz.shape[2]
    width = proj.shape[1] // 3
    heads = width // DH
    model = tok.shape[2]
    bufs = (wz, wy, wo)

    local = [
        pltpu.make_async_copy(tok_in, tok.at[0], local_sem.at[0]),
        pltpu.make_async_copy(qkv_in.at[:, pl.ds(0, z_cols)], wz.at[f], local_sem.at[1]),
        pltpu.make_async_copy(
            qkv_in.at[:, pl.ds(z_cols, wy.shape[2])], wy.at[f], local_sem.at[2]
        ),
        pltpu.make_async_copy(out_in, wo.at[f], local_sem.at[3]),
        pltpu.make_async_copy(act_in, act, local_sem.at[4]),
    ]
    for copy in local:
        copy.start()

    barrier = pltpu.get_barrier_semaphore()
    for k in range(1, shards):
        pl.semaphore_signal(barrier, inc=1, device_id={"fsdp": lax.rem(f + k, shards)},
                            device_id_type=pl.DeviceIdType.MESH)
    for k in range(1, seqs):
        pl.semaphore_signal(barrier, inc=1, device_id={"seq": lax.rem(s + k, seqs)},
                            device_id_type=pl.DeviceIdType.MESH)

    def shard_copy(kind, origin, way):
        if way == UP:
            target = lax.rem(f + PAIR, shards)
        elif way == DOWN:
            target = lax.rem(f + shards - PAIR, shards)
        else:
            target = a * PAIR + (1 - b)
        return pltpu.make_async_remote_copy(
            src_ref=bufs[kind].at[origin],
            dst_ref=bufs[kind].at[origin],
            send_sem=send_sem.at[way, kind, origin],
            recv_sem=recv_sem.at[kind, origin],
            device_id={"fsdp": target},
            device_id_type=pl.DeviceIdType.MESH,
        )

    def arrived(kind, origin):
        shard_copy(kind, origin, ACROSS).wait_recv()

    def send_up(kind, origin):
        @pl.when(a < length - 1)
        def _():
            shard_copy(kind, origin, UP).start()

    def send_down(kind, origin):
        @pl.when(a > 0)
        def _():
            shard_copy(kind, origin, DOWN).start()

    def at_distance(d, act_on):
        @pl.when(a - d >= 0)
        def _():
            act_on(0, a - d)

        @pl.when(jnp.logical_and(a + d < length, d > 0))
        def _():
            act_on(1, a + d)

    def tok_copy(k):
        return pltpu.make_async_remote_copy(
            src_ref=tok.at[0],
            dst_ref=tok.at[seqs - k],
            send_sem=tok_send.at[k],
            recv_sem=tok_recv.at[seqs - k],
            device_id={"seq": lax.rem(s + k, seqs)},
            device_id_type=pl.DeviceIdType.MESH,
        )

    for copy in local[:4]:
        copy.wait()
    pl.semaphore_wait(barrier, shards - 1 + seqs - 1)

    shard_copy(PAIR_QKV, f, ACROSS).start()
    shard_copy(LINE_QKV, f, ACROSS).start()
    send_up(LINE_QKV, f)
    send_down(LINE_QKV, f)
    for k in range(1, seqs):
        tok_copy(k).start()

    def norm_slot(k):
        step = 32

        def piece(i, carry):
            part = pl.ds(pl.multiple_of(i * step, step), step)
            values = normalize(tok[k, part, :].astype(F32)).astype(BF16)
            dest = pl.ds(pl.multiple_of(k * rows + i * step, step), step)
            for g in range(shards):
                nrm[g, dest, :] = values[:, g * depth:(g + 1) * depth]
            return carry

        lax.fori_loop(0, rows // step, piece, 0)

    norm_slot(0)
    for g in range(shards):
        own_tok[g] = tok[0, :, g * cols:(g + 1) * cols]
    table = table_ref[...]
    bins = bias_ref.shape[1]
    onehot = (lax.broadcasted_iota(jnp.int32, (bins, table.shape[1]), 0) == table).astype(F32)
    bias_row[...] = jnp.dot(
        bias_ref[...], onehot, preferred_element_type=F32, precision=lax.Precision.HIGHEST
    )
    acc_z[...] = jnp.zeros_like(acc_z)
    acc_y[...] = jnp.zeros_like(acc_y)

    half = acc_z.shape[0] // 2

    def add_z(origin):
        def piece(i, carry):
            part = pl.ds(pl.multiple_of(i * half, half), half)
            acc_z[part, :] += jnp.dot(nrm[origin, part, :], wz[origin],
                                      preferred_element_type=F32)
            return carry

        lax.fori_loop(0, 2, piece, 0)

    def add_y(origin):
        acc_y[...] += jnp.dot(nrm[origin], wy[origin], preferred_element_type=F32)

    def line_forward(kind, d):
        def forward(side, o):
            origin = o * PAIR + b
            arrived(kind, origin)
            if side == 0:
                send_up(kind, origin)
            else:
                send_down(kind, origin)
            shard_copy(kind, origin, ACROSS).start()

        at_distance(d, forward)

    turn = max(length - 2, 1)

    def line_step(d, carry):
        line_forward(LINE_QKV, d)

        @pl.when(d == turn)
        def _():
            send_up(PAIR_QKV, f)
            send_down(PAIR_QKV, f)
            other = a * PAIR + (1 - b)
            arrived(PAIR_QKV, other)
            send_up(PAIR_QKV, other)
            send_down(PAIR_QKV, other)

        @pl.when(d == 1)
        def _():
            for k in range(1, seqs):
                tok_copy(seqs - k).wait_recv()
                norm_slot(k)
            add_z(f)

        at_distance(d, lambda side, o: add_z(o * PAIR + b))
        return carry

    lax.fori_loop(1, length, line_step, 0)
    shard_copy(LINE_OUT, f, ACROSS).start()

    add_y(f)
    add_y(a * PAIR + (1 - b))

    def across_z(d):
        def use(side, o):
            origin = o * PAIR + (1 - b)
            arrived(LINE_QKV, origin)
            add_z(origin)

        at_distance(d, use)

    def pair_step(d, carry):
        for column in (b, 1 - b):
            def forward(side, o):
                origin = o * PAIR + column
                arrived(PAIR_QKV, origin)
                if side == 0:
                    send_up(PAIR_QKV, origin)
                else:
                    send_down(PAIR_QKV, origin)

            at_distance(d, forward)

        @pl.when(d == turn)
        def _():
            send_up(LINE_OUT, f)
            send_down(LINE_OUT, f)

        def use(side, o):
            add_y(o * PAIR)
            add_y(o * PAIR + 1)

        at_distance(d, use)
        across_z(d - 1)
        return carry

    lax.fori_loop(1, length, pair_step, 0)
    across_z(length - 1)

    proj[:, 0:z_cols] = acc_z[...].astype(BF16)
    proj[:, z_cols:] = acc_y[...].astype(BF16)
    scale = 1.0 / math.sqrt(DH)

    def head_step(h, carry):
        start = pl.multiple_of(h * DH, DH)
        query = proj[:, pl.ds(start, DH)]
        key = proj[:, pl.ds(width + start, DH)]
        value = proj[:, pl.ds(2 * width + start, DH)]
        total = None
        mixed = None
        for k in range(seqs):
            part = slice(k * rows, (k + 1) * rows)
            score = lax.dot_general(query, key[part], (((1,), (1,)), ((), ())),
                                    preferred_element_type=F32)
            keep = valid_ref[0, lax.rem(s + k, seqs)].astype(F32)
            weight = jnp.exp(score * scale) * keep
            part_total = jnp.sum(weight, axis=-1, keepdims=True)
            part_mixed = jnp.dot(weight.astype(BF16), value[part], preferred_element_type=F32)
            total = part_total if total is None else total + part_total
            mixed = part_mixed if mixed is None else mixed + part_mixed
        att[:, pl.ds(start, DH)] = (mixed / total).astype(BF16)
        return carry

    lax.fori_loop(0, heads, head_step, 0)

    def part_copy(k, block):
        return pltpu.make_async_remote_copy(
            src_ref=part_out.at[k - 1, block],
            dst_ref=part_in.at[seqs - k - 1, block],
            send_sem=part_send.at[k - 1, block],
            recv_sem=part_recv.at[seqs - k - 1, block],
            device_id={"seq": lax.rem(s + k, seqs)},
            device_id_type=pl.DeviceIdType.MESH,
        )

    def out_block(block):
        product = jnp.dot(att[...], wo[block], preferred_element_type=F32)
        for k in range(1, seqs):
            part_out[k - 1, block] = product[k * rows:(k + 1) * rows].astype(BF16)
        own_part[block] = product[0:rows]
        for k in range(1, seqs):
            part_copy(k, block).start()

    out_block(f)

    def across_out(d):
        def use(side, o):
            origin = o * PAIR + (1 - b)
            arrived(LINE_OUT, origin)
            out_block(origin)

        at_distance(d, use)

    def out_step(d, carry):
        line_forward(LINE_OUT, d)
        at_distance(d, lambda side, o: out_block(o * PAIR + b))
        across_out(d - 1)
        return carry

    lax.fori_loop(1, length, out_step, 0)
    across_out(length - 1)

    def finish(block, carry):
        total = own_part[block]
        for k in range(1, seqs):
            part_copy(seqs - k, block).wait_recv()
            total = total + part_in[k - 1, block].astype(F32)
        rounded = (own_tok[block].astype(F32) + total).astype(BF16)
        hid[block] = rounded
        col_sum[block] = jnp.sum(rounded.astype(F32), axis=0, keepdims=True)
        return carry

    lax.fori_loop(0, shards, finish, 0)

    pooled = normalize(
        jnp.concatenate([col_sum[g] for g in range(shards)], axis=-1) * (1.0 / rows)
    )
    lanes = row_tile.shape[1]
    for i in range(model // lanes):
        row_tile[i:i + 1, :] = pooled[:, i * lanes:(i + 1) * lanes]
    pool_tile[f] = row_tile[...].astype(BF16)

    def pool_copy(k):
        target = lax.rem(f + k, shards)
        return pltpu.make_async_remote_copy(
            src_ref=pool_tile.at[f],
            dst_ref=pool_tile.at[f],
            send_sem=pool_send.at[k],
            recv_sem=pool_recv.at[k],
            device_id={"fsdp": target},
            device_id_type=pl.DeviceIdType.MESH,
        )

    for k in range(1, shards):
        pool_copy(k).start()
    for g in range(shards):
        hidden_ref[:, g * cols:(g + 1) * cols] = hid[g]
    local[4].wait()

    for k in range(1, seqs):
        tok_copy(k).wait_send()

    def drain(o, carry):
        own = o * PAIR + b
        other = o * PAIR + (1 - b)
        for kind in (LINE_QKV, LINE_OUT):
            shard_copy(kind, own, ACROSS).wait_send()

        @pl.when(jnp.logical_and(o <= a, a < length - 1))
        def _():
            for kind in (LINE_QKV, LINE_OUT, PAIR_QKV):
                shard_copy(kind, own, UP).wait_send()
            shard_copy(PAIR_QKV, other, UP).wait_send()

        @pl.when(jnp.logical_and(o >= a, a > 0))
        def _():
            for kind in (LINE_QKV, LINE_OUT, PAIR_QKV):
                shard_copy(kind, own, DOWN).wait_send()
            shard_copy(PAIR_QKV, other, DOWN).wait_send()

        return carry

    lax.fori_loop(0, length, drain, 0)
    shard_copy(PAIR_QKV, f, ACROSS).wait_send()

    def drain_parts(block, carry):
        for k in range(1, seqs):
            part_copy(k, block).wait_send()
        return carry

    lax.fori_loop(0, shards, drain_parts, 0)

    for k in range(1, shards):
        pool_copy(k).wait_recv()
    pool_wide[...] = pool_tile[...].astype(F32)
    for i in range(model // lanes):
        pool_rows[:, i * lanes:(i + 1) * lanes] = pool_wide[:, i, :]
    logits_ref[...] = (
        jnp.dot(pool_rows[...].astype(BF16), act[...], preferred_element_type=F32)
        + bias_row[...]
    )
    for k in range(1, shards):
        pool_copy(k).wait_send()


def per_device(shards, seqs, tokens, frame_valid, w_qkv, w_out, w_act, class_table, cam_bias):
    rows, model = tokens.shape[3], tokens.shape[4]
    depth, width = w_qkv.shape[0], w_qkv.shape[2]
    cols, classes = w_out.shape[1], w_act.shape[1]
    span = seqs * rows
    y_cols = 3 * width // 4
    z_cols = 3 * width - y_cols
    lanes = 128
    any_spec = pl.BlockSpec(memory_space=pl.ANY)
    vmem_spec = pl.BlockSpec(memory_space=pltpu.VMEM)
    hidden, logits = pl.pallas_call(
        functools.partial(layer_kernel, shards, seqs),
        out_shape=(
            jax.ShapeDtypeStruct((rows, model), BF16),
            jax.ShapeDtypeStruct((shards, classes), F32),
        ),
        in_specs=[
            any_spec,
            pl.BlockSpec(memory_space=pltpu.SMEM),
            any_spec, any_spec, any_spec, vmem_spec, vmem_spec,
        ],
        out_specs=(vmem_spec, vmem_spec),
        scratch_shapes=[
            pltpu.VMEM((seqs, rows, model), BF16),
            pltpu.VMEM((shards, span, depth), BF16),
            pltpu.VMEM((shards, rows, cols), BF16),
            pltpu.VMEM((shards, depth, z_cols), BF16),
            pltpu.VMEM((shards, depth, y_cols), BF16),
            pltpu.VMEM((shards, width, cols), BF16),
            pltpu.VMEM((model, classes), BF16),
            pltpu.VMEM((span, z_cols), F32),
            pltpu.VMEM((span, y_cols), F32),
            pltpu.VMEM((span, 3 * width), BF16),
            pltpu.VMEM((span, width), BF16),
            pltpu.VMEM((shards, rows, cols), F32),
            pltpu.VMEM((seqs - 1, shards, rows, cols), BF16),
            pltpu.VMEM((seqs - 1, shards, rows, cols), BF16),
            pltpu.VMEM((shards, rows, cols), BF16),
            pltpu.VMEM((shards, 1, cols), F32),
            pltpu.VMEM((model // lanes, lanes), F32),
            pltpu.VMEM((shards, model // lanes, lanes), BF16),
            pltpu.VMEM((shards, model // lanes, lanes), F32),
            pltpu.VMEM((shards, model), F32),
            pltpu.VMEM((1, classes), F32),
            pltpu.SemaphoreType.DMA((5,)),
            pltpu.SemaphoreType.DMA((3, 3, shards)),
            pltpu.SemaphoreType.DMA((3, shards)),
            pltpu.SemaphoreType.DMA((seqs,)),
            pltpu.SemaphoreType.DMA((seqs,)),
            pltpu.SemaphoreType.DMA((seqs - 1, shards)),
            pltpu.SemaphoreType.DMA((seqs - 1, shards)),
            pltpu.SemaphoreType.DMA((shards,)),
            pltpu.SemaphoreType.DMA((shards,)),
        ],
        compiler_params=pltpu.CompilerParams(
            collective_id=0, has_side_effects=True, vmem_limit_bytes=60 * 1024 * 1024
        ),
        name="layer",
    )(
        tokens.reshape(rows, model),
        frame_valid.reshape(1, seqs),
        w_qkv.reshape(depth, 3 * width),
        w_out,
        w_act,
        class_table.reshape(1, classes),
        cam_bias.reshape(1, cam_bias.shape[0]),
    )
    return (
        hidden.reshape(1, 1, 1, rows, model),
        logits.reshape(shards, 1, 1, classes),
    )


def solution(mesh):
    in_specs = (
        P(("groups", "fsdp"), "sub", "seq", None, None),
        P(("groups", "fsdp"), "sub", None),
        P("fsdp", None, "seq"),
        P("seq", "fsdp"),
        P(None, "fsdp"),
        P("fsdp"),
        P(),
    )
    out_specs = (P(("groups", "fsdp"), "sub", "seq", None, None), P("groups", "sub", "seq", "fsdp"))
    body = functools.partial(per_device, mesh.shape["fsdp"], mesh.shape["seq"])
    return jax.shard_map(
        body, mesh=mesh, in_specs=in_specs, out_specs=out_specs, check_vma=False
    )
```

time: 283 us -> 117 us (0.41)
  waiting for transfers between devices: 209 us -> 0 us
  Pallas kernels: 0 us -> 110 us
  blocking collectives: 30.7 us -> 0 us
  matrix products: 17.1 us -> 0 us
  between operations: 15.2 us -> 0.64 us
  other arithmetic: 8.18 us -> 0 us
    all_gather x3 -> x0, waiting for transfers between devices: 165 us -> none  [the longest x1 102 us: per_device(): full_qkv = lax.all_gather(w_qkv, 'fsdp', axis=0, tiled=True)]
    pallas_call x0 -> x1, Pallas kernels: none -> 110 us  [per_device(): pl.pallas_call(functools.partial(layer_kernel, shards, seqs), out_shape=(...]
    reduce_scatter x1 -> x0, waiting for transfers between devices: 42.4 us -> none  [per_device(): lax.psum_scatter(jnp.dot(frame_major, full_out, preferred_element_type=jn...]
    all_gather x1 -> x0, blocking collectives: 30.7 us -> none  [per_device(): lax.all_gather(pooled, 'fsdp', axis=0, tiled=True)]
    dot_general x6 -> x0, matrix products: 17.1 us -> none  [the longest x1 6.89 us: per_device(): jnp.einsum('wsd,dcn->wscn', window_rows, full_qkv, preferred_element_type...]
    convert_element_type x4 -> x0, other arithmetic: 4.35 us -> none  [the longest x1 2.18 us: per_device(): hidden_out = hidden.astype(jnp.bfloat16)]
    reduce_sum x5 -> x0, other arithmetic: 3.82 us -> none  [the longest x2 1.93 us: normalize(): spread = jnp.mean(jnp.square(values - centre), axis=-1, keepdims=True)]
  transfers between devices with their start and end apart: 4 -> 0, of which waited for: 4 -> 0; matrix products, arithmetic and copies ran while one was open for 4% -> 0% of each run, Pallas kernels for 0% -> 0%
where the time goes in v1:
time: 117 us
  Pallas kernels  110 us (94%)
  local copies, waits for them, and re-layouts  5.85 us (5%)
    pallas_call x1, Pallas kernels, per_device(): pl.pallas_call(functools.partial(layer_kernel, shards, seqs), out_shape=(...  110 us
    unnamed x3, local copies, waits for them, and re-layouts  4.69 us

profile of v1, /device:TPU:0, one launch (start us, length us, event | category | flops | bytes accessed | tf_op | source)
XLA Modules:
  0.0 116.8 jit_solution(6452076620454834677)
XLA Ops:
  0.6 1.4 %copy.11 = bf16[256,3,512]{0,2,1:T(8,128)(2,1)S(1)} copy(bf16[256,3,512]{2,0,1:T(8,128)(2,1)} %param.9) | data formatting | bytes 1572864 | tf_op args[2]
  2.0 1.2 copy.12.qkv_in
  3.2 110.3 %layer.1 = (bf16[128,2048]{1,0:T(8,128)(2,1)}, f32[8,1024]{1,0:T(8,128)}) custom-call(bf16[128,2048]{1,0:T(8,128)(2,1)} %bitcast.9, s32[1,4]{1,0:T(1,128)} %bitcast.12, bf16[256,1536]{1,0:T(8,128)(2,1)} %copy.12.qkv_in, bf16[512,256]{1,0:T(8,128)(2,1)} %out_in.1, bf16[2048,1024]{1,0:T(8,128)(2,1)} %act_in.1, s32[1,1024]{1,0:T(1,128)} %bitcast.11, ...), custom_call_target="tpu_custom_call" | custom-call | tf_op jit(solution)/shard_map/layer/pallas_call | solution.py:400
  113.5 1.4 %copy.13 = f32[8,1,1,1024]{3,2,1,0:T(1,128)} copy(f32[8,1,1,1024]{3,0,2,1:T(8,128)} %bitcast.10) | data formatting | bytes 65536
  115.0 1.9 %copy.15 = bf16[1,1,1,128,2048]{4,3,2,1,0:T(8,128)(2,1)} copy(bf16[1,1,1,128,2048]{4,3,2,1,0:T(8,128)(2,1)} %bitcast.8) | data formatting | bytes 1048576

commit v2 on v1

--- a/solution.py
+++ b/solution.py
@@ -28,7 +28,7 @@
     tok_in, valid_ref, qkv_in, out_in, act_in, table_ref, bias_ref,
     hidden_ref, logits_ref,
     tok, nrm, own_tok, wz, wy, wo, act, acc_z, acc_y, proj, att, own_part,
-    part_out, part_in, hid, col_sum, row_tile, pool_tile, pool_wide, pool_rows, bias_row,
+    part_out, part_in, hid, col_sum, row_tile, pool_tile, pool_wide, pool_rows, bias_row, hidden_tile,
     local_sem, send_sem, recv_sem, tok_send, tok_recv, part_send, part_recv, pool_send, pool_recv,
 ):
     f = lax.axis_index("fsdp")
@@ -47,13 +47,24 @@
 
     local = [
         pltpu.make_async_copy(tok_in, tok.at[0], local_sem.at[0]),
-        pltpu.make_async_copy(qkv_in.at[:, pl.ds(0, z_cols)], wz.at[f], local_sem.at[1]),
         pltpu.make_async_copy(
-            qkv_in.at[:, pl.ds(z_cols, wy.shape[2])], wy.at[f], local_sem.at[2]
+            qkv_in.at[0], wz.at[f, :, pl.ds(0, width)], local_sem.at[1]
         ),
-        pltpu.make_async_copy(out_in, wo.at[f], local_sem.at[3]),
-        pltpu.make_async_copy(act_in, act, local_sem.at[4]),
+        pltpu.make_async_copy(
+            qkv_in.at[1], wz.at[f, :, pl.ds(width, width)], local_sem.at[2]
+        ),
+        pltpu.make_async_copy(
+            qkv_in.at[2, :, pl.ds(0, z_cols - 2 * width)],
+            wz.at[f, :, pl.ds(2 * width, z_cols - 2 * width)],
+            local_sem.at[3],
+        ),
+        pltpu.make_async_copy(
+            qkv_in.at[2, :, pl.ds(z_cols - 2 * width, wy.shape[2])], wy.at[f], local_sem.at[4]
+        ),
+        pltpu.make_async_copy(out_in, wo.at[f], local_sem.at[5]),
+        pltpu.make_async_copy(act_in, act, local_sem.at[6]),
     ]
+    hidden_copy = pltpu.make_async_copy(hidden_tile, hidden_ref, local_sem.at[7])
     for copy in local:
         copy.start()
 
@@ -113,7 +124,7 @@
             device_id_type=pl.DeviceIdType.MESH,
         )
 
-    for copy in local[:4]:
+    for copy in local[:6]:
         copy.wait()
     pl.semaphore_wait(barrier, shards - 1 + seqs - 1)
 
@@ -295,16 +306,7 @@
 
         at_distance(d, use)
 
-    def out_step(d, carry):
-        line_forward(LINE_OUT, d)
-        at_distance(d, lambda side, o: out_block(o * PAIR + b))
-        across_out(d - 1)
-        return carry
-
-    lax.fori_loop(1, length, out_step, 0)
-    across_out(length - 1)
-
-    def finish(block, carry):
+    def finish(block):
         total = own_part[block]
         for k in range(1, seqs):
             part_copy(seqs - k, block).wait_recv()
@@ -312,9 +314,28 @@
         rounded = (own_tok[block].astype(F32) + total).astype(BF16)
         hid[block] = rounded
         col_sum[block] = jnp.sum(rounded.astype(F32), axis=0, keepdims=True)
+
+    def finish_at(d, column):
+        at_distance(d, lambda side, o: finish(o * PAIR + column))
+
+    def out_step(d, carry):
+        line_forward(LINE_OUT, d)
+        at_distance(d, lambda side, o: out_block(o * PAIR + b))
+        finish_at(d - 1, b)
+
+        @pl.when(d >= 2)
+        def _():
+            finish_at(d - 2, 1 - b)
+
+        across_out(d - 1)
         return carry
 
-    lax.fori_loop(0, shards, finish, 0)
+    lax.fori_loop(1, length, out_step, 0)
+    finish_at(length - 1, b)
+    finish_at(length - 2, 1 - b)
+    across_out(length - 1)
+    finish_at(length - 1, 1 - b)
+
 
     pooled = normalize(
         jnp.concatenate([col_sum[g] for g in range(shards)], axis=-1) * (1.0 / rows)
@@ -338,8 +359,9 @@
     for k in range(1, shards):
         pool_copy(k).start()
     for g in range(shards):
-        hidden_ref[:, g * cols:(g + 1) * cols] = hid[g]
-    local[4].wait()
+        hidden_tile[:, g * cols:(g + 1) * cols] = hid[g]
+    hidden_copy.start()
+    local[6].wait()
 
     for k in range(1, seqs):
         tok_copy(k).wait_send()
@@ -385,6 +407,7 @@
     )
     for k in range(1, shards):
         pool_copy(k).wait_send()
+    hidden_copy.wait()
 
 
 def per_device(shards, seqs, tokens, frame_valid, w_qkv, w_out, w_act, class_table, cam_bias):
@@ -392,7 +415,7 @@
     depth, width = w_qkv.shape[0], w_qkv.shape[2]
     cols, classes = w_out.shape[1], w_act.shape[1]
     span = seqs * rows
-    y_cols = 3 * width // 4
+    y_cols = width // 2
     z_cols = 3 * width - y_cols
     lanes = 128
     any_spec = pl.BlockSpec(memory_space=pl.ANY)
@@ -408,7 +431,7 @@
             pl.BlockSpec(memory_space=pltpu.SMEM),
             any_spec, any_spec, any_spec, vmem_spec, vmem_spec,
         ],
-        out_specs=(vmem_spec, vmem_spec),
+        out_specs=(any_spec, vmem_spec),
         scratch_shapes=[
             pltpu.VMEM((seqs, rows, model), BF16),
             pltpu.VMEM((shards, span, depth), BF16),
@@ -431,7 +454,8 @@
             pltpu.VMEM((shards, model // lanes, lanes), F32),
             pltpu.VMEM((shards, model), F32),
             pltpu.VMEM((1, classes), F32),
-            pltpu.SemaphoreType.DMA((5,)),
+            pltpu.VMEM((rows, model), BF16),
+            pltpu.SemaphoreType.DMA((8,)),
             pltpu.SemaphoreType.DMA((3, 3, shards)),
             pltpu.SemaphoreType.DMA((3, shards)),
             pltpu.SemaphoreType.DMA((seqs,)),
@@ -448,7 +472,7 @@
     )(
         tokens.reshape(rows, model),
         frame_valid.reshape(1, seqs),
-        w_qkv.reshape(depth, 3 * width),
+        jnp.transpose(w_qkv, (1, 0, 2)),
         w_out,
         w_act,
         class_table.reshape(1, classes),

time: 117 us -> 110 us (0.940)
  Pallas kernels: 110 us -> 106 us
  local copies, waits for them, and re-layouts: 5.85 us -> 3.29 us
    pallas_call x1, Pallas kernels: 110 us -> 106 us  [per_device(): pl.pallas_call(functools.partial(layer_kernel, shards, seqs), out_shape=(...]
    unnamed x3 -> x2, local copies, waits for them, and re-layouts: 4.69 us -> 3.29 us
where the time goes in v2:
time: 110 us
  Pallas kernels  106 us (96%)
  local copies, waits for them, and re-layouts  3.29 us (3%)
    pallas_call x1, Pallas kernels, per_device(): pl.pallas_call(functools.partial(layer_kernel, shards, seqs), out_shape=(...  106 us
    unnamed x2, local copies, waits for them, and re-layouts  3.29 us

profile of v2, /device:TPU:0, one launch (start us, length us, event | category | flops | bytes accessed | tf_op | source)
XLA Modules:
  0.0 110.0 jit_solution(14713592736989428157)
XLA Ops:
  0.6 106.0 %layer.1 = (bf16[128,2048]{1,0:T(8,128)(2,1)}, f32[8,1024]{1,0:T(8,128)}) custom-call(bf16[128,2048]{1,0:T(8,128)(2,1)} %bitcast.9, s32[1,4]{1,0:T(1,128)} %bitcast.12, bf16[3,256,512]{2,1,0:T(8,128)(2,1)} %bitcast.7, bf16[512,256]{1,0:T(8,128)(2,1)} %out_in.1, bf16[2048,1024]{1,0:T(8,128)(2,1)} %act_in.1, s32[1,1024]{1,0:T(1,128)} %bitcast.11, ...), custom_call_target="tpu_custom_call" | custom-call | tf_op jit(solution)/shard_map/layer/pallas_call | solution.py:423
  106.7 1.4 %copy.9 = f32[8,1,1,1024]{3,2,1,0:T(1,128)} copy(f32[8,1,1,1024]{3,0,2,1:T(8,128)} %bitcast.10) | data formatting | bytes 65536
  108.1 1.9 %copy.11 = bf16[1,1,1,128,2048]{4,3,2,1,0:T(8,128)(2,1)} copy(bf16[1,1,1,128,2048]{4,3,2,1,0:T(8,128)(2,1)} %bitcast.8) | data formatting | bytes 1048576

commit v3 on v2

--- a/solution.py
+++ b/solution.py
@@ -28,8 +28,8 @@
     tok_in, valid_ref, qkv_in, out_in, act_in, table_ref, bias_ref,
     hidden_ref, logits_ref,
     tok, nrm, own_tok, wz, wy, wo, act, acc_z, acc_y, proj, att, own_part,
-    part_out, part_in, hid, col_sum, row_tile, pool_tile, pool_wide, pool_rows, bias_row, hidden_tile,
-    local_sem, send_sem, recv_sem, tok_send, tok_recv, part_send, part_recv, pool_send, pool_recv,
+    mate_out, mate_in, part_out, part_in, hid, col_sum, row_tile, pool_tile, pool_wide, pool_rows, bias_row, hidden_tile,
+    local_sem, send_sem, recv_sem, tok_send, tok_recv, mate_send, mate_recv, part_send, part_recv, pool_send, pool_recv,
 ):
     f = lax.axis_index("fsdp")
     s = lax.axis_index("seq")
@@ -278,25 +278,53 @@
 
     lax.fori_loop(0, heads, head_step, 0)
 
-    def part_copy(k, block):
+    odd = s % 2
+    mate = s + 1 - 2 * odd
+    folds = seqs // 2
+
+    def mate_copy(block):
         return pltpu.make_async_remote_copy(
-            src_ref=part_out.at[k - 1, block],
-            dst_ref=part_in.at[seqs - k - 1, block],
-            send_sem=part_send.at[k - 1, block],
-            recv_sem=part_recv.at[seqs - k - 1, block],
-            device_id={"seq": lax.rem(s + k, seqs)},
+            src_ref=mate_out.at[block],
+            dst_ref=mate_in.at[block],
+            send_sem=mate_send.at[block],
+            recv_sem=mate_recv.at[block],
+            device_id={"seq": mate},
             device_id_type=pl.DeviceIdType.MESH,
         )
 
+    def part_copy(j, block):
+        return pltpu.make_async_remote_copy(
+            src_ref=part_out.at[j - 1, block],
+            dst_ref=part_in.at[folds - j - 1, block],
+            send_sem=part_send.at[j - 1, block],
+            recv_sem=part_recv.at[folds - j - 1, block],
+            device_id={"seq": lax.rem(s + 2 * j, seqs)},
+            device_id_type=pl.DeviceIdType.MESH,
+        )
+
     def out_block(block):
         product = jnp.dot(att[...], wo[block], preferred_element_type=F32)
-        for k in range(1, seqs):
-            part_out[k - 1, block] = product[k * rows:(k + 1) * rows].astype(BF16)
-        own_part[block] = product[0:rows]
-        for k in range(1, seqs):
-            part_copy(k, block).start()
+
+        def slot(k):
+            return product[k * rows:(k + 1) * rows]
+
+        for j in range(folds):
+            mate_out[block, j] = jnp.where(
+                odd == 0, slot(2 * j + 1), slot((2 * j - 1) % seqs)
+            ).astype(BF16)
+            own_part[block, j] = slot(2 * j)
+        mate_copy(block).start()
+
+    def fold_block(block):
+        mate_copy(block).wait_recv()
+        for j in range(1, folds):
+            part_out[j - 1, block] = (
+                own_part[block, j] + mate_in[block, j].astype(F32)
+            ).astype(BF16)
+            part_copy(j, block).start()
 
     out_block(f)
+    fold_block(f)
 
     def across_out(d):
         def use(side, o):
@@ -305,12 +333,13 @@
             out_block(origin)
 
         at_distance(d, use)
+        at_distance(d, lambda side, o: fold_block(o * PAIR + (1 - b)))
 
     def finish(block):
-        total = own_part[block]
-        for k in range(1, seqs):
-            part_copy(seqs - k, block).wait_recv()
-            total = total + part_in[k - 1, block].astype(F32)
+        total = own_part[block, 0] + mate_in[block, 0].astype(F32)
+        for j in range(1, folds):
+            part_copy(folds - j, block).wait_recv()
+            total = total + part_in[j - 1, block].astype(F32)
         rounded = (own_tok[block].astype(F32) + total).astype(BF16)
         hid[block] = rounded
         col_sum[block] = jnp.sum(rounded.astype(F32), axis=0, keepdims=True)
@@ -321,6 +350,7 @@
     def out_step(d, carry):
         line_forward(LINE_OUT, d)
         at_distance(d, lambda side, o: out_block(o * PAIR + b))
+        at_distance(d, lambda side, o: fold_block(o * PAIR + b))
         finish_at(d - 1, b)
 
         @pl.when(d >= 2)
@@ -390,8 +420,9 @@
     shard_copy(PAIR_QKV, f, ACROSS).wait_send()
 
     def drain_parts(block, carry):
-        for k in range(1, seqs):
-            part_copy(k, block).wait_send()
+        mate_copy(block).wait_send()
+        for j in range(1, folds):
+            part_copy(j, block).wait_send()
         return carry
 
     lax.fori_loop(0, shards, drain_parts, 0)
@@ -415,6 +446,7 @@
     depth, width = w_qkv.shape[0], w_qkv.shape[2]
     cols, classes = w_out.shape[1], w_act.shape[1]
     span = seqs * rows
+    folds = seqs // 2
     y_cols = width // 2
     z_cols = 3 * width - y_cols
     lanes = 128
@@ -444,9 +476,11 @@
             pltpu.VMEM((span, y_cols), F32),
             pltpu.VMEM((span, 3 * width), BF16),
             pltpu.VMEM((span, width), BF16),
-            pltpu.VMEM((shards, rows, cols), F32),
-            pltpu.VMEM((seqs - 1, shards, rows, cols), BF16),
-            pltpu.VMEM((seqs - 1, shards, rows, cols), BF16),
+            pltpu.VMEM((shards, folds, rows, cols), F32),
+            pltpu.VMEM((shards, folds, rows, cols), BF16),
+            pltpu.VMEM((shards, folds, rows, cols), BF16),
+            pltpu.VMEM((folds - 1, shards, rows, cols), BF16),
+            pltpu.VMEM((folds - 1, shards, rows, cols), BF16),
             pltpu.VMEM((shards, rows, cols), BF16),
             pltpu.VMEM((shards, 1, cols), F32),
             pltpu.VMEM((model // lanes, lanes), F32),
@@ -460,8 +494,10 @@
             pltpu.SemaphoreType.DMA((3, shards)),
             pltpu.SemaphoreType.DMA((seqs,)),
             pltpu.SemaphoreType.DMA((seqs,)),
-            pltpu.SemaphoreType.DMA((seqs - 1, shards)),
-            pltpu.SemaphoreType.DMA((seqs - 1, shards)),
+            pltpu.SemaphoreType.DMA((shards,)),
+            pltpu.SemaphoreType.DMA((shards,)),
+            pltpu.SemaphoreType.DMA((folds - 1, shards)),
+            pltpu.SemaphoreType.DMA((folds - 1, shards)),
             pltpu.SemaphoreType.DMA((shards,)),
             pltpu.SemaphoreType.DMA((shards,)),
         ],

time: 110 us -> 111 us (level)
  no operation moved by 1% of the time
where the time goes in v3:
time: 111 us
  Pallas kernels  107 us (96%)
  local copies, waits for them, and re-layouts  3.29 us (3%)
    pallas_call x1, Pallas kernels, per_device(): pl.pallas_call(functools.partial(layer_kernel, shards, seqs), out_shape=(...  107 us
    unnamed x2, local copies, waits for them, and re-layouts  3.29 us

profile of v3, /device:TPU:0, one launch (start us, length us, event | category | flops | bytes accessed | tf_op | source)
XLA Modules:
  0.0 111.0 jit_solution(16604122728364369148)
XLA Ops:
  0.6 107.1 %layer.1 = (bf16[128,2048]{1,0:T(8,128)(2,1)}, f32[8,1024]{1,0:T(8,128)}) custom-call(bf16[128,2048]{1,0:T(8,128)(2,1)} %bitcast.9, s32[1,4]{1,0:T(1,128)} %bitcast.12, bf16[3,256,512]{2,1,0:T(8,128)(2,1)} %bitcast.7, bf16[512,256]{1,0:T(8,128)(2,1)} %out_in.1, bf16[2048,1024]{1,0:T(8,128)(2,1)} %act_in.1, s32[1,1024]{1,0:T(1,128)} %bitcast.11, ...), custom_call_target="tpu_custom_call" | custom-call | tf_op jit(solution)/shard_map/layer/pallas_call | solution.py:455
  107.7 1.4 %copy.9 = f32[8,1,1,1024]{3,2,1,0:T(1,128)} copy(f32[8,1,1,1024]{3,0,2,1:T(8,128)} %bitcast.10) | data formatting | bytes 65536
  109.1 1.9 %copy.11 = bf16[1,1,1,128,2048]{4,3,2,1,0:T(8,128)(2,1)} copy(bf16[1,1,1,128,2048]{4,3,2,1,0:T(8,128)(2,1)} %bitcast.8) | data formatting | bytes 1048576

commit v4 on v2

--- a/solution.py
+++ b/solution.py
@@ -257,7 +257,7 @@
     scale = 1.0 / math.sqrt(DH)
 
     def head_step(h, carry):
-        start = pl.multiple_of(h * DH, DH)
+        start = h * DH
         query = proj[:, pl.ds(start, DH)]
         key = proj[:, pl.ds(width + start, DH)]
         value = proj[:, pl.ds(2 * width + start, DH)]
@@ -276,7 +276,8 @@
         att[:, pl.ds(start, DH)] = (mixed / total).astype(BF16)
         return carry
 
-    lax.fori_loop(0, heads, head_step, 0)
+    for h in range(heads):
+        head_step(h, 0)
 
     def part_copy(k, block):
         return pltpu.make_async_remote_copy(
@@ -401,10 +402,12 @@
     pool_wide[...] = pool_tile[...].astype(F32)
     for i in range(model // lanes):
         pool_rows[:, i * lanes:(i + 1) * lanes] = pool_wide[:, i, :]
-    logits_ref[...] = (
+    logits = (
         jnp.dot(pool_rows[...].astype(BF16), act[...], preferred_element_type=F32)
         + bias_row[...]
     )
+    for g in range(shards):
+        logits_ref[g] = logits[g:g + 1]
     for k in range(1, shards):
         pool_copy(k).wait_send()
     hidden_copy.wait()
@@ -424,7 +427,7 @@
         functools.partial(layer_kernel, shards, seqs),
         out_shape=(
             jax.ShapeDtypeStruct((rows, model), BF16),
-            jax.ShapeDtypeStruct((shards, classes), F32),
+            jax.ShapeDtypeStruct((shards, 1, classes), F32),
         ),
         in_specs=[
             any_spec,

time: 110 us -> 109 us (level)
  no operation moved by 1% of the time
where the time goes in v4:
time: 109 us
  Pallas kernels  105 us (96%)
  local copies, waits for them, and re-layouts  3.26 us (3%)
    pallas_call x1, Pallas kernels, per_device(): pl.pallas_call(functools.partial(layer_kernel, shards, seqs), out_shape=(...  105 us
    unnamed x2, local copies, waits for them, and re-layouts  3.26 us

profile of v4, /device:TPU:0, one launch (start us, length us, event | category | flops | bytes accessed | tf_op | source)
XLA Modules:
  0.0 108.9 jit_solution(15366769136481789386)
XLA Ops:
  0.6 105.0 %layer.1 = (bf16[128,2048]{1,0:T(8,128)(2,1)}, f32[8,1,1024]{2,1,0:T(1,128)}) custom-call(bf16[128,2048]{1,0:T(8,128)(2,1)} %bitcast.11, s32[1,4]{1,0:T(1,128)} %bitcast.14, bf16[3,256,512]{2,1,0:T(8,128)(2,1)} %bitcast.9, bf16[512,256]{1,0:T(8,128)(2,1)} %out_in.1, bf16[2048,1024]{1,0:T(8,128)(2,1)} %act_in.1, s32[1,1024]{1,0:T(1,128)} %bitcast.13, ...), custom_call_target="tpu_custom_call" | custom-call | tf_op jit(solution)/shard_map/layer/pallas_call | solution.py:426
  105.6 1.9 %copy.12 = bf16[1,1,1,128,2048]{4,3,2,1,0:T(8,128)(2,1)} copy(bf16[1,1,1,128,2048]{4,3,2,1,0:T(8,128)(2,1)} %bitcast.10) | data formatting | bytes 1048576
  107.5 1.4 %copy.13 = f32[8,1,1,1024]{3,2,1,0:T(1,128)} copy(f32[8,1,1,1024]{3,2,1,0:T(1,128)} %bitcast.12) | data formatting | bytes 65536
